TPU v7x, 128 devices: a whole 4x4x4 slice. The times are simulated.
128 devices in a mesh: ctx: 8 (over y, core), tp: 8 (over x_lo, z), pp: 2 (over x_hi).
Axes of the slice: x: 4 (x_hi: 2, x_lo: 2; x = x_hi * 2 + x_lo), y: 4, z: 4, core: 2. Of those that a mesh axis runs over, the one named last changes fastest.
Arguments:
- queries: bfloat16 [2, 2048, 12288], P('pp', 'ctx', 'tp'), may hold values from -8 to 8
- latents: bfloat16 [2, 2048, 576], P('pp', ('ctx', 'tp')), may hold values from -8 to 8
- latent_gain: float32 [2, 512], P('pp'), may hold values from 0.5 to 2
- w_ukv: bfloat16 [2, 512, 16384], P('pp', None, 'tp'), may hold values from -0.25 to 0.25
- w_o: bfloat16 [2, 8192, 7168], P('pp', 'tp'), may hold values from -0.1875 to 0.1875
- residual: bfloat16 [2, 2048, 7168], P('pp', ('ctx', 'tp')), may hold values from -3 to 3
- block_order: int32 [2, 16], P('pp'), may hold values from 0 to 15, each once within a row
Outputs:
- handed: bfloat16 [2, 2048, 7168], P('pp', ('ctx', 'tp'))
Inputs may be any that keep to these rules, and one draw needn't show every extreme that they name: `block_order`: each row names each of the 16 sequence blocks once.
All inputs are finite; a program needn't handle non-finite values.
Results may differ from a plain program's by a relative error of at most 0.02.
Values may be sent and summed in bfloat16 or wider, within the bound.
A program may use at most 128 MiB of HBM per device.

v0:
```python
import jax
import jax.numpy as jnp
from jax import lax
from jax.sharding import PartitionSpec as P

NOPE = 128
ROPE = 64
VDIM = 128
LATENT = 512
score_scale = 0.135


def passed_along(value, axis, steps):
    count = lax.axis_size(axis)
    pairs = [(source, (source + steps) % count) for source in range(count)]
    return lax.ppermute(value, axis, pairs)


def rotate(values, places):
    middle = values.shape[-1] // 2
    freqs = 10000.0 ** (-(jnp.arange(middle).astype(jnp.float32) * 2.0 / values.shape[-1]))
    angles = places[..., None] * freqs
    first_half = values[..., :middle]
    second_half = values[..., middle:]
    return jnp.concatenate(
        [
            first_half * jnp.cos(angles) - second_half * jnp.sin(angles),
            first_half * jnp.sin(angles) + second_half * jnp.cos(angles),
        ],
        axis=-1,
    )


def place_rows(order_row, first, count, block_len):
    row_ids = first + jnp.arange(count, dtype=jnp.int32)
    owners = row_ids // block_len
    table = jnp.arange(order_row.shape[0], dtype=jnp.int32)
    base = jnp.sum(jnp.where(owners[:, None] == table[None, :], order_row[None, :], 0), axis=1)
    return base * block_len + row_ids % block_len


def local(queries, latents, latent_gain, w_ukv, w_o, residual, block_order):
    order_row = block_order[0]
    tp_count = lax.axis_size("tp")
    tok_dev = queries.shape[1]
    block_len = tok_dev // 2
    lat_rows = latents.shape[1]
    heads_here = w_o.shape[1] // VDIM
    query_places = place_rows(order_row, lax.axis_index("ctx") * tok_dev, tok_dev, block_len)
    query_all = queries[0].reshape(tok_dev, heads_here, NOPE + ROPE)
    query_nope = query_all[..., :NOPE]
    query_rope = rotate(
        query_all[..., NOPE:].astype(jnp.float32), query_places.astype(jnp.float32)[:, None]
    ).astype(jnp.bfloat16)
    own_first = (lax.axis_index("ctx") * tp_count + lax.axis_index("tp")) * lat_rows
    own_places = place_rows(order_row, own_first, lat_rows, block_len)
    latent_rows = latents[0].astype(jnp.float32)
    compressed = latent_rows[:, :LATENT]
    scale_rows = lax.rsqrt(jnp.mean(compressed * compressed, axis=-1, keepdims=True) + 1e-06)
    normed = (compressed * scale_rows * latent_gain[0][None, :]).astype(jnp.bfloat16)
    own_rope = rotate(latent_rows[:, LATENT:], own_places.astype(jnp.float32)).astype(jnp.bfloat16)
    own_keys = jnp.concatenate([normed, own_rope], axis=-1)
    up_weights = w_ukv[0]

    def expand(latent_part):
        produced = jnp.dot(latent_part, up_weights, preferred_element_type=jnp.float32).astype(
            jnp.bfloat16
        )
        return produced.reshape(latent_part.shape[0], heads_here, NOPE + VDIM)

    piece = lax.all_gather(own_keys, ("ctx", "tp"), axis=0, tiled=True)
    make_keys = lambda: (expand(piece[:, :LATENT]), piece[:, LATENT:])
    key_places = place_rows(order_row, jnp.int32(0), piece.shape[0], block_len)
    running_max = jnp.full((tok_dev, heads_here), -1e30, jnp.float32)
    key_value, key_rope = make_keys()
    scores = (
        jnp.einsum(
            "thd,nhd->thn", query_nope, key_value[..., :NOPE], preferred_element_type=jnp.float32
        )
        + jnp.einsum("thr,nr->thn", query_rope, key_rope, preferred_element_type=jnp.float32)
    ) * score_scale
    allowed = (key_places[None, :] <= query_places[:, None])[:, None, :]
    scores = jnp.where(allowed, scores, -1e30)
    new_max = jnp.maximum(running_max, jnp.max(scores, axis=-1))
    weights = jnp.where(allowed, jnp.exp(scores - new_max[..., None]), 0.0)
    new_total = jnp.sum(weights, axis=-1)
    new_sum = jnp.einsum(
        "thn,nhd->thd",
        weights.astype(jnp.bfloat16),
        key_value[..., NOPE:],
        preferred_element_type=jnp.float32,
    )
    attention = (
        (new_sum / new_total[..., None]).astype(jnp.bfloat16).reshape(tok_dev, heads_here * VDIM)
    )
    out_weights = w_o[0]
    summed = lax.psum_scatter(
        jnp.dot(attention, out_weights, preferred_element_type=jnp.float32).astype(jnp.bfloat16),
        "tp",
        scatter_dimension=0,
        tiled=True,
    ).astype(jnp.float32)
    mixed = (summed + residual[0].astype(jnp.float32)).astype(jnp.bfloat16)
    handed = passed_along(mixed, "pp", 1)
    return handed[None]


def solution(mesh):
    in_specs = (
        P("pp", "ctx", "tp"),
        P("pp", ("ctx", "tp"), None),
        P("pp", None),
        P("pp", None, "tp"),
        P("pp", "tp", None),
        P("pp", ("ctx", "tp"), None),
        P("pp", None),
    )
    out_specs = P("pp", ("ctx", "tp"), None)
    return jax.shard_map(local, mesh=mesh, in_specs=in_specs, out_specs=out_specs, check_vma=False)
```

profile of v0, /device:TPU:0, one launch (start us, length us, event | category | flops | bytes accessed | tf_op | source)
XLA Modules:
  0.0 292.4 jit_solution(18152602769886171369)
XLA Ops:
  6.6 0.9 bitcast_convert_fusion
  7.5 0.7 select_reduce_fusion.2
  8.3 0.1 multiply_reduce_fusion
  8.4 0.1 fusion.38
  8.5 0.8 multiply_convert_fusion
  9.3 0.7 pad_maximum_fusion
  10.1 1.4 copy.26
  11.5 0.8 select_reduce_fusion.1
  12.3 0.8 select_reduce_fusion
  13.1 0.2 multiply_cosine_fusion
  13.3 0.8 subtract_convert_fusion
  14.1 0.4 broadcast_compare_fusion
  14.5 155.7 %all-gather.2.cloned.1.call-done = bf16[2048,576]{1,0:T(8,128)(2,1)} async-done(((bf16[32,576]{1,0:T(8,128)(2,1)}), bf16[2048,576]{1,0:T(8,128)(2,1)}) %all-gather.2.cloned.1.call-update) | async-done | bytes 2359312 | tf_op jit(solution)/shard_map/all_gather | solution.py:71
  170.2 8.3 %convolution_convert_fusion = bf16[2048,2048]{0,1:T(8,128)(2,1)} fusion(bf16[2048,576]{1,0:T(8,128)(2,1)} %all-gather.2.cloned.1.call-done, bf16[1,512,2048]{2,1,0:T(8,128)(2,1)S(1)} %copy-done), kind=kOutput, calls=%fused_computation.13 | convolution fusion | flops 4299161600 | bytes 12582912 | tf_op jit(solution)/shard_map/dot_general | solution.py:66
  178.6 4.7 %fusion.14 = f32[8,2048,256]{2,1,0:T(8,128)S(1)} fusion(bf16[2048,8,256]{0,2,1:T(8,128)(2,1)} %bitcast.39, bf16[256,8,192]{0,2,1:T(8,128)(2,1)} %bitcast.38), kind=kOutput, calls=%fused_computation.14 | convolution fusion | flops 1073741824 | bytes 21495808 | tf_op jit(solution)/shard_map/thd,nhd->thn/dot_general | solution.py:77
  183.3 8.8 %fusion.57 = (f32[256,8]{0,1:T(8,128)S(1)}, f32[256,8,2048]{0,2,1:T(8,128)}) fusion(bf16[256,8,32]{0,2,1:T(8,128)(2,1)S(1)} %copy-done.4, bf16[256,8,32]{0,2,1:T(8,128)(2,1)S(1)} %copy-done.3, bf16[2048,576]{1,0:T(8,128)(2,1)} %all-gather.2.cloned.1.call-done, f32[8,2048,256]{2,1,0:T(8,128)S(1)} %fusion.14, pred[256,2048]{0,1:T(8,128)(4,1)S(1)} %broadcast_compare_fusion), kind=kOutput, calls=%fused_computation.89 | convolution fusion | flops 554170368 | bytes 34873344 | tf_op jit(solution)/shard_map/thr,nr->thn/dot_general | solution.py:80
  192.1 8.6 %fusion.4 = f32[256,8]{0,1:T(8,128)S(1)} fusion(f32[256,8,2048]{0,2,1:T(8,128)} %get-tuple-element.14, f32[256,8]{0,1:T(8,128)S(1)} %broadcast_maximum_fusion, pred[256,2048]{0,1:T(8,128)(4,1)S(1)} %broadcast_compare_fusion), kind=kLoop, calls=%fused_computation.6 | loop fusion | flops 12580864 | bytes 17317888 | tf_op jit(solution)/shard_map/reduce_sum | solution.py:86
  200.8 10.1 %divide_convert_fusion = bf16[256,8,128]{0,2,1:T(8,128)(2,1)S(1)} fusion(f32[256,8,2048]{0,2,1:T(8,128)} %get-tuple-element.14, f32[256,8]{0,1:T(8,128)S(1)} %broadcast_maximum_fusion, pred[256,2048]{0,1:T(8,128)(4,1)S(1)} %broadcast_compare_fusion, bf16[2048,8,256]{0,2,1:T(8,128)(2,1)} %bitcast.40, f32[256,8]{0,1:T(8,128)S(1)} %fusion.4), kind=kOutput, calls=%fused_computation.20 | convolution fusion | flops 1086849024 | bytes 22036480 | tf_op jit(solution)/shard_map/thn,nhd->thd/dot_general | solution.py:87
  210.9 11.0 %fusion.6 = bf16[256,7168]{1,0:T(8,128)(2,1)} fusion(bf16[256,1024]{0,1:T(8,128)(2,1)S(1)} %bitcast.41, bf16[1,1024,7168]{2,1,0:T(8,128)(2,1)} %param.11), kind=kOutput, calls=%fused_computation.8 | convolution fusion | flops 3759931392 | bytes 18874368 | tf_op jit(solution)/shard_map/dot_general | solution.py:98
  221.9 49.7 %reduce-scatter.2.cloned.1.call-done = bf16[32,7168]{1,0:T(8,128)(2,1)} async-done(((bf16[256,7168]{1,0:T(8,128)(2,1)}), bf16[32,7168]{1,0:T(8,128)(2,1)}) %reduce-scatter.2.cloned.1.call-update) | async-done | bytes 458768 | tf_op jit(solution)/shard_map/reduce_scatter | solution.py:97
  271.6 1.1 fusion.28
  272.7 2.7 collective-permute-start
  275.4 9.4 %collective-permute-done = bf16[32,7168]{1,0:T(8,128)(2,1)S(1)} collective-permute-done((bf16[32,7168]{1,0:T(8,128)(2,1)S(1)}, bf16[32,7168]{1,0:T(8,128)(2,1)S(1)}, u32[]{:S(2)}, u32[]{:S(2)}) %collective-permute-start) | collective-permute-done | bytes 458784 | tf_op jit(solution)/shard_map/ppermute | solution.py:16
  284.8 0.8 copy.37
  (26 shorter events, 0.2 us)
Async XLA Ops:
  6.5 163.7 %copy-start = (bf16[1,512,2048]{2,1,0:T(8,128)(2,1)S(1)}, bf16[1,512,2048]{2,1,0:T(8,128)(2,1)}, u32[]{:S(2)}) copy-start(bf16[1,512,2048]{2,1,0:T(8,128)(2,1)} %param.10) | copy-start | bytes 6291460
  6.5 163.7 %all-gather.2.cloned.1.call-start = ((), (), s32[]{:S(2)}) async-start(), calls=%async_computation.1 | async-start | bytes 2662400 | tf_op jit(solution)/shard_map/all_gather | solution.py:71
  10.0 261.6 %reduce-scatter.2.cloned.1.call-start = ((), (), s32[]{:S(2)}) async-start(), calls=%async_computation.2 | async-start | bytes 4128768 | tf_op jit(solution)/shard_map/reduce_scatter | solution.py:97
  11.5 167.1 %copy-start.2 = (bf16[1,256,1536]{1,2,0:T(8,128)(2,1)}, bf16[1,256,1536]{1,2,0:T(8,128)(2,1)S(1)}, u32[]{:S(2)}) copy-start(bf16[1,256,1536]{1,2,0:T(8,128)(2,1)S(1)} %copy.26) | copy-start | bytes 2359300
  178.5 4.7 %copy-start.3 = (bf16[256,8,32]{0,2,1:T(8,128)(2,1)S(1)}, bf16[256,8,32]{0,2,1:T(8,128)(2,1)}, u32[]{:S(2)}) copy-start(bf16[256,8,32]{0,2,1:T(8,128)(2,1)} %get-tuple-element.7) | copy-start | bytes 393220
  178.6 4.7 %copy-start.4 = (bf16[256,8,32]{0,2,1:T(8,128)(2,1)S(1)}, bf16[256,8,32]{0,2,1:T(8,128)(2,1)}, u32[]{:S(2)}) copy-start(bf16[256,8,32]{0,2,1:T(8,128)(2,1)} %get-tuple-element.8) | copy-start | bytes 393220
  210.9 74.7 %copy-start.1 = (bf16[1,512,2048]{2,1,0:T(8,128)(2,1)S(1)}, bf16[1,512,2048]{2,1,0:T(8,128)(2,1)}, u32[]{:S(2)}) copy-start(bf16[1,512,2048]{2,1,0:T(8,128)(2,1)} %param.10) | copy-start | bytes 6291460
  210.9 60.7 %copy-start.5 = (bf16[1,32,7168]{2,1,0:T(8,128)(2,1)S(1)}, bf16[1,32,7168]{2,1,0:T(8,128)(2,1)}, u32[]{:S(2)}) copy-start(bf16[1,32,7168]{2,1,0:T(8,128)(2,1)} %param.12) | copy-start | bytes 1376260
  272.7 12.1 %collective-permute-start = (bf16[32,7168]{1,0:T(8,128)(2,1)S(1)}, bf16[32,7168]{1,0:T(8,128)(2,1)S(1)}, u32[]{:S(2)}, u32[]{:S(2)}) collective-permute-start(bf16[32,7168]{1,0:T(8,128)(2,1)S(1)} %fusion.28), channel_id=1, source_target_pairs={{0,1},{1,0},{2,3},{3,2},{4,5},{5,4},{6,7},{7,6},{8,9},{9,8},{10,11... | collective-permute-start | bytes 1376264 | tf_op jit(solution)/shard_map/ppermute | solution.py:16
Sparse Core Ops, SparseCore 0:
  10.1 160.0 all-gather.1
  222.0 49.5 reduce-scatter.1
where the time goes:
time: 293 us; the launch traced here: 292 us
  waiting for transfers between devices  215 us (73%)
  matrix products  42.9 us (15%)
  other arithmetic  16.2 us (6%)
  between operations  13.5 us (5%)
    all_gather x1, waiting for transfers between devices, local(): piece = lax.all_gather(own_keys, ('ctx', 'tp'), axis=0, tiled=True)  156 us
    reduce_scatter x1, waiting for transfers between devices, local(): lax.psum_scatter(jnp.dot(attention, out_weights, preferred_element_type=j...  49.7 us
    dot_general x1, matrix products, local(): jnp.dot(attention, out_weights, preferred_element_type=jnp.float32)  11 us
    dot_general x1, matrix products, local(): jnp.einsum('thn,nhd->thd', weights.astype(jnp.bfloat16), key_value[..., N...  10.1 us
    ppermute x1, waiting for transfers between devices, passed_along(): return lax.ppermute(value, axis, pairs)  9.41 us
    dot_general x1, matrix products, local(): jnp.einsum('thr,nr->thn', query_rope, key_rope, preferred_element_type=jn...  8.81 us
    reduce_sum x1, other arithmetic, local(): new_total = jnp.sum(weights, axis=-1)  8.63 us
    dot_general x1, matrix products, expand(): jnp.dot(latent_part, up_weights, preferred_element_type=jnp.float32)  8.34 us
  transfers between devices with their start and end apart: 3, of which 3 were waited for; matrix products, arithmetic and copies ran while one was open for 2% of the time, Pallas kernels for 0%

commit v1 on v0

--- a/solution.py
+++ b/solution.py
@@ -68,7 +68,10 @@
         )
         return produced.reshape(latent_part.shape[0], heads_here, NOPE + VDIM)
 
-    piece = lax.all_gather(own_keys, ("ctx", "tp"), axis=0, tiled=True)
+    loads_answer = lambda chunk, mesh_name, k_dim: jnp.concatenate(
+        lax.all_to_all(jnp.stack([chunk] * lax.axis_size(mesh_name)), mesh_name, 0, 0), axis=k_dim
+    )
+    piece = loads_answer(own_keys, ("ctx", "tp"), 0)
     make_keys = lambda: (expand(piece[:, :LATENT]), piece[:, LATENT:])
     key_places = place_rows(order_row, jnp.int32(0), piece.shape[0], block_len)
     running_max = jnp.full((tok_dev, heads_here), -1e30, jnp.float32)

time: 293 us -> 176 us (0.60)
  waiting for transfers between devices: 215 us -> 87.9 us
  starting transfers between devices: 2.77 us -> 13 us
    all_gather x1 -> x0, waiting for transfers between devices: 156 us -> none  [local(): piece = lax.all_gather(own_keys, ('ctx', 'tp'), axis=0, tiled=True)]
    all_to_all x0 -> x1, waiting for transfers between devices: none -> 30.2 us  [local(): lax.all_to_all(jnp.stack([chunk] * lax.axis_size(mesh_name)), mesh_name,...]
    all_to_all x0 -> x1, starting transfers between devices: none -> 10.2 us  [local(): lax.all_to_all(jnp.stack([chunk] * lax.axis_size(mesh_name)), mesh_name,...]
where the time goes in v1:
time: 176 us
  waiting for transfers between devices  87.9 us (50%)
  matrix products  43 us (24%)
  other arithmetic  14.3 us (8%)
  between operations  13.5 us (8%)
  starting transfers between devices  13 us (7%)
  local copies, waits for them, and re-layouts  3.91 us (2%)
    reduce_scatter x1, waiting for transfers between devices, local(): lax.psum_scatter(jnp.dot(attention, out_weights, preferred_element_type=j...  48.3 us
    all_to_all x1, waiting for transfers between devices, local(): lax.all_to_all(jnp.stack([chunk] * lax.axis_size(mesh_name)), mesh_name,...  30.2 us
    dot_general x1, matrix products, local(): jnp.dot(attention, out_weights, preferred_element_type=jnp.float32)  11 us
    all_to_all x1, starting transfers between devices, local(): lax.all_to_all(jnp.stack([chunk] * lax.axis_size(mesh_name)), mesh_name,...  10.2 us
    dot_general x1, matrix products, local(): jnp.einsum('thn,nhd->thd', weights.astype(jnp.bfloat16), key_value[..., N...  10.1 us
    ppermute x1, waiting for transfers between devices, passed_along(): return lax.ppermute(value, axis, pairs)  9.34 us
    dot_general x1, matrix products, local(): jnp.einsum('thr,nr->thn', query_rope, key_rope, preferred_element_type=jn...  8.82 us
    reduce_sum x1, other arithmetic, local(): new_total = jnp.sum(weights, axis=-1)  8.63 us
  transfers between devices with their start and end apart: 3, of which 3 were waited for; matrix products, arithmetic and copies ran while one was open for 2% of the time, Pallas kernels for 0%

profile of v1, /device:TPU:0, one launch (start us, length us, event | category | flops | bytes accessed | tf_op | source)
XLA Modules:
  0.0 175.6 jit_solution(10296650977998473844)
XLA Ops:
  6.6 0.9 bitcast_convert_fusion
  7.5 0.7 select_reduce_fusion.2
  8.3 0.1 multiply_reduce_fusion
  8.4 0.1 fusion.38
  8.5 0.8 multiply_convert_fusion
  9.4 1.7 stack.2
  11.1 10.2 %all-to-all-start = ((bf16[64,32,576]{2,1,0:T(8,128)(2,1)}), bf16[64,32,576]{2,1,0:T(8,128)(2,1)}, u32[]{:S(2)}, u32[]{:S(2)}) async-start(bf16[64,32,576]{2,1,0:T(8,128)(2,1)} %stack.2), calls=%async_computation | async-start | bytes 5242880 | tf_op jit(solution)/shard_map/all_to_all | solution.py:72
  21.3 1.4 copy.20
  22.9 0.1 select_reduce_fusion
  23.0 0.2 multiply_cosine_fusion
  23.3 0.8 subtract_convert_fusion
  24.0 0.4 broadcast_compare_fusion
  24.5 30.2 %all-to-all-done = bf16[64,32,576]{2,1,0:T(8,128)(2,1)} async-done(((bf16[64,32,576]{2,1,0:T(8,128)(2,1)}), bf16[64,32,576]{2,1,0:T(8,128)(2,1)}, u32[]{:S(2)}, u32[]{:S(2)}) %all-to-all-start) | async-done | bytes 2359328 | tf_op jit(solution)/shard_map/all_to_all | solution.py:72
  54.7 8.3 %convolution_convert_fusion = bf16[2048,2048]{0,1:T(8,128)(2,1)} fusion(bf16[2048,576]{1,0:T(8,128)(2,1)} %bitcast.4, bf16[1,512,2048]{2,1,0:T(8,128)(2,1)S(1)} %copy-done), kind=kOutput, calls=%fused_computation.13 | convolution fusion | flops 4299161600 | bytes 12582912 | tf_op jit(solution)/shard_map/dot_general | solution.py:66
  63.1 4.7 %fusion.14 = f32[8,2048,256]{2,1,0:T(8,128)S(1)} fusion(bf16[2048,8,256]{0,2,1:T(8,128)(2,1)} %bitcast.40, bf16[256,8,192]{0,2,1:T(8,128)(2,1)} %bitcast.39), kind=kOutput, calls=%fused_computation.14 | convolution fusion | flops 1073741824 | bytes 21495808 | tf_op jit(solution)/shard_map/thd,nhd->thn/dot_general | solution.py:80
  67.8 8.8 %fusion.57 = (f32[256,8]{0,1:T(8,128)S(1)}, f32[256,8,2048]{0,2,1:T(8,128)}) fusion(bf16[256,8,32]{0,2,1:T(8,128)(2,1)S(1)} %copy-done.4, bf16[256,8,32]{0,2,1:T(8,128)(2,1)S(1)} %copy-done.3, bf16[2048,576]{1,0:T(8,128)(2,1)} %bitcast.4, f32[8,2048,256]{2,1,0:T(8,128)S(1)} %fusion.14, pred[256,2048]{0,1:T(8,128)(4,1)S(1)} %broadcast_compare_fusion), kind=kOutput, calls=%fused_computation.89 | convolution fusion | flops 554170368 | bytes 34873344 | tf_op jit(solution)/shard_map/thr,nr->thn/dot_general | solution.py:83
  76.7 8.6 %fusion.4 = f32[256,8]{0,1:T(8,128)S(1)} fusion(f32[256,8,2048]{0,2,1:T(8,128)} %get-tuple-element.14, f32[256,8]{0,1:T(8,128)S(1)} %broadcast_maximum_fusion, pred[256,2048]{0,1:T(8,128)(4,1)S(1)} %broadcast_compare_fusion), kind=kLoop, calls=%fused_computation.6 | loop fusion | flops 12580864 | bytes 17317888 | tf_op jit(solution)/shard_map/reduce_sum | solution.py:89
  85.3 10.1 %divide_convert_fusion = bf16[256,8,128]{0,2,1:T(8,128)(2,1)S(1)} fusion(f32[256,8,2048]{0,2,1:T(8,128)} %get-tuple-element.14, f32[256,8]{0,1:T(8,128)S(1)} %broadcast_maximum_fusion, pred[256,2048]{0,1:T(8,128)(4,1)S(1)} %broadcast_compare_fusion, bf16[2048,8,256]{0,2,1:T(8,128)(2,1)} %bitcast.41, f32[256,8]{0,1:T(8,128)S(1)} %fusion.4), kind=kOutput, calls=%fused_computation.20 | convolution fusion | flops 1086849024 | bytes 22036480 | tf_op jit(solution)/shard_map/thn,nhd->thd/dot_general | solution.py:90
  95.4 11.0 %fusion.6 = bf16[256,7168]{1,0:T(8,128)(2,1)} fusion(bf16[256,1024]{0,1:T(8,128)(2,1)S(1)} %bitcast.42, bf16[1,1024,7168]{2,1,0:T(8,128)(2,1)} %param.11), kind=kOutput, calls=%fused_computation.8 | convolution fusion | flops 3759931392 | bytes 18874368 | tf_op jit(solution)/shard_map/dot_general | solution.py:101
  106.4 48.3 %reduce-scatter.2.cloned.1.call-done = bf16[32,7168]{1,0:T(8,128)(2,1)} async-done(((bf16[256,7168]{1,0:T(8,128)(2,1)}), bf16[32,7168]{1,0:T(8,128)(2,1)}) %reduce-scatter.2.cloned.1.call-update) | async-done | bytes 458768 | tf_op jit(solution)/shard_map/reduce_scatter | solution.py:100
  154.7 1.1 fusion.28
  155.8 2.7 %collective-permute-start = (bf16[32,7168]{1,0:T(8,128)(2,1)S(1)}, bf16[32,7168]{1,0:T(8,128)(2,1)S(1)}, u32[]{:S(2)}, u32[]{:S(2)}) collective-permute-start(bf16[32,7168]{1,0:T(8,128)(2,1)S(1)} %fusion.28), channel_id=1, source_target_pairs={{0,1},{1,0},{2,3},{3,2},{4,5},{5,4},{6,7},{7,6},{8,9},{9,8},{10,11... | collective-permute-start | bytes 1376264 | tf_op jit(solution)/shard_map/ppermute | solution.py:16
  158.6 9.3 %collective-permute-done = bf16[32,7168]{1,0:T(8,128)(2,1)S(1)} collective-permute-done((bf16[32,7168]{1,0:T(8,128)(2,1)S(1)}, bf16[32,7168]{1,0:T(8,128)(2,1)S(1)}, u32[]{:S(2)}, u32[]{:S(2)}) %collective-permute-start) | collective-permute-done | bytes 458784 | tf_op jit(solution)/shard_map/ppermute | solution.py:16
  167.9 0.8 copy.31
  (28 shorter events, 0.4 us)
Async XLA Ops:
  6.5 48.2 %copy-start = (bf16[1,512,2048]{2,1,0:T(8,128)(2,1)S(1)}, bf16[1,512,2048]{2,1,0:T(8,128)(2,1)}, u32[]{:S(2)}) copy-start(bf16[1,512,2048]{2,1,0:T(8,128)(2,1)} %param.10) | copy-start | bytes 6291460
  6.5 16.2 %copy-start.6 = (s32[1,16]{1,0:T(1,128)S(1)}, s32[1,16]{1,0:T(1,128)}, u32[]{:S(2)}) copy-start(s32[1,16]{1,0:T(1,128)} %param.13) | copy-start | bytes 196
  11.1 43.6 %all-to-all-start = ((bf16[64,32,576]{2,1,0:T(8,128)(2,1)}), bf16[64,32,576]{2,1,0:T(8,128)(2,1)}, u32[]{:S(2)}, u32[]{:S(2)}) async-start(bf16[64,32,576]{2,1,0:T(8,128)(2,1)} %stack.2), calls=%async_computation | async-start | bytes 5242880 | tf_op jit(solution)/shard_map/all_to_all | solution.py:72
  21.3 133.4 %reduce-scatter.2.cloned.1.call-start = ((), (), s32[]{:S(2)}) async-start(), calls=%async_computation.2 | async-start | bytes 4128768 | tf_op jit(solution)/shard_map/reduce_scatter | solution.py:100
  22.7 40.3 %copy-start.2 = (bf16[1,256,1536]{1,2,0:T(8,128)(2,1)}, bf16[1,256,1536]{1,2,0:T(8,128)(2,1)S(1)}, u32[]{:S(2)}) copy-start(bf16[1,256,1536]{1,2,0:T(8,128)(2,1)S(1)} %copy.20) | copy-start | bytes 2359300
  63.1 4.7 %copy-start.3 = (bf16[256,8,32]{0,2,1:T(8,128)(2,1)S(1)}, bf16[256,8,32]{0,2,1:T(8,128)(2,1)}, u32[]{:S(2)}) copy-start(bf16[256,8,32]{0,2,1:T(8,128)(2,1)} %get-tuple-element.7) | copy-start | bytes 393220
  63.1 4.7 %copy-start.4 = (bf16[256,8,32]{0,2,1:T(8,128)(2,1)S(1)}, bf16[256,8,32]{0,2,1:T(8,128)(2,1)}, u32[]{:S(2)}) copy-start(bf16[256,8,32]{0,2,1:T(8,128)(2,1)} %get-tuple-element.8) | copy-start | bytes 393220
  95.4 73.3 %copy-start.1 = (bf16[1,512,2048]{2,1,0:T(8,128)(2,1)S(1)}, bf16[1,512,2048]{2,1,0:T(8,128)(2,1)}, u32[]{:S(2)}) copy-start(bf16[1,512,2048]{2,1,0:T(8,128)(2,1)} %param.10) | copy-start | bytes 6291460
  95.4 59.3 %copy-start.5 = (bf16[1,32,7168]{2,1,0:T(8,128)(2,1)S(1)}, bf16[1,32,7168]{2,1,0:T(8,128)(2,1)}, u32[]{:S(2)}) copy-start(bf16[1,32,7168]{2,1,0:T(8,128)(2,1)} %param.12) | copy-start | bytes 1376260
  155.8 12.1 %collective-permute-start = (bf16[32,7168]{1,0:T(8,128)(2,1)S(1)}, bf16[32,7168]{1,0:T(8,128)(2,1)S(1)}, u32[]{:S(2)}, u32[]{:S(2)}) collective-permute-start(bf16[32,7168]{1,0:T(8,128)(2,1)S(1)} %fusion.28), channel_id=1, source_target_pairs={{0,1},{1,0},{2,3},{3,2},{4,5},{5,4},{6,7},{7,6},{8,9},{9,8},{10,11... | collective-permute-start | bytes 1376264 | tf_op jit(solution)/shard_map/ppermute | solution.py:16
Sparse Core Ops, SparseCore 0:
  106.5 48.1 reduce-scatter.1
